TPU v7x, 32 devices: a whole 2x2x4 slice. The times are simulated.
32 devices in a mesh: dp: 8 (over y, x, core), tensor: 4 (over z).
Axes of the slice: x: 2, y: 2, z: 4, core: 2. Of those that a mesh axis runs over, the one named last changes fastest.
Arguments:
- tokens: bfloat16 [5120, 1024], P(('dp', 'tensor')), may hold values from -6 to 6
- cotangent: float32 [5120, 1024], P(('dp', 'tensor')), may hold values from -6 to 6
- image_group: int32 [7], replicated, may hold values from 0 to 7, as said below
- first_norm_gain_param: float32 [1024], P(('dp', 'tensor')), may hold values from 0.1 to 1.9
- first_norm_bias: float32 [1024], P(('dp', 'tensor')), may hold values from -3 to 3
- w_qkv: bfloat16 [1024, 3072], P('dp', 'tensor'), may hold values from -0.1875 to 0.1875
- qv_bias: float32 [2048], P(('dp', 'tensor')), may hold values from -3 to 3
- w_out: bfloat16 [1024, 1024], P('tensor', 'dp'), may hold values from -1 to 1
- out_bias: float32 [1024], P(('dp', 'tensor')), may hold values from -3 to 3
- second_norm_gain_param: float32 [1024], P(('dp', 'tensor')), may hold values from 0.1 to 1.9
- second_norm_bias: float32 [1024], P(('dp', 'tensor')), may hold values from -3 to 3
- w_up: bfloat16 [1024, 4096], P('dp', 'tensor'), may hold values from -0.1875 to 0.1875
- up_bias: float32 [4096], P(('dp', 'tensor')), may hold values from -3 to 3
- w_down: bfloat16 [4096, 1024], P('tensor', 'dp'), may hold values from -0.09375 to 0.09375
- down_bias: float32 [1024], P(('dp', 'tensor')), may hold values from -3 to 3
Outputs:
- output: bfloat16 [5120, 1024], P(('dp', 'tensor'))
- layer_input_gradient: float32 [5120, 1024], P(('dp', 'tensor'))
- ln1_gain_grad: float32 [1024], P(('dp', 'tensor'))
- ln1_bias_grad: float32 [1024], P(('dp', 'tensor'))
- w_qkv_grad: float32 [1024, 3072], P('dp', 'tensor')
- qv_bias_grad: float32 [2048], P(('dp', 'tensor'))
- w_out_grad: float32 [1024, 1024], P('tensor', 'dp')
- out_bias_grad: float32 [1024], P(('dp', 'tensor'))
- ln2_gain_grad: float32 [1024], P(('dp', 'tensor'))
- ln2_bias_grad: float32 [1024], P(('dp', 'tensor'))
- w_up_grad: float32 [1024, 4096], P('dp', 'tensor')
- up_bias_grad: float32 [4096], P(('dp', 'tensor'))
- w_down_grad: float32 [4096, 1024], P('tensor', 'dp')
- down_bias_grad: float32 [1024], P(('dp', 'tensor'))
Inputs may be any that keep to these rules, and one draw needn't show every extreme that they name: Group image_group[i] holds image i; 1 group hold 0 images and all others 1.
All inputs are finite; a program needn't handle non-finite values.
Results may differ from a plain program's by a relative error of at most 0.015.
Values may be sent and summed in bfloat16 or wider, within the bound.
A program may use at most 128 MiB of HBM per device.

v0:
```python
import jax
import jax.numpy as jnp
from jax import lax
from jax.sharding import PartitionSpec as P

D = 1024
HEAD_DIM = 64
FF = 4096
SEQ = 577
SEQ_PAD = 640


EPS = 1e-06
NEG_LARGE = -1e30
ROOT_HALF = 0.7071067811865476
INV_ROOT_TAU = 0.3989422804014327


def apply_layer_norm(values, norm_gain_vector, norm_shift_vector):
    average = jnp.mean(values, axis=1, keepdims=True)
    mean_removed = values - average
    variance = jnp.mean(mean_removed * mean_removed, axis=1, keepdims=True)
    inverse_deviation = lax.rsqrt(variance + EPS)
    standardized_rows = mean_removed * inverse_deviation
    return (
        standardized_rows * norm_gain_vector + norm_shift_vector,
        standardized_rows,
        inverse_deviation,
    )


def layer_norm_backward(incoming_gradient, standardized_rows, inverse_deviation, norm_gain_vector):
    gain_scaled_gradient = incoming_gradient * norm_gain_vector
    return inverse_deviation * (
        gain_scaled_gradient
        - jnp.mean(gain_scaled_gradient, axis=1, keepdims=True)
        - standardized_rows
        * jnp.mean(gain_scaled_gradient * standardized_rows, axis=1, keepdims=True)
    )


def gelu_value(hidden):
    return 0.5 * hidden * (1.0 + jax.scipy.special.erf(hidden * ROOT_HALF))


def gelu_slope(hidden):
    return 0.5 * (
        1.0 + jax.scipy.special.erf(hidden * ROOT_HALF)
    ) + hidden * INV_ROOT_TAU * jnp.exp(-0.5 * hidden * hidden)


def left_product(first, second):
    return lax.dot_general(
        first, second, (((0,), (0,)), ((), ())), preferred_element_type=jnp.float32
    )


def right_product(first, second):
    return lax.dot_general(
        first, second, (((1,), (1,)), ((), ())), preferred_element_type=jnp.float32
    )


def gather_rows(values):
    return lax.all_gather(values, "tensor", axis=0, tiled=True)


def scatter_rows(values):
    return lax.psum_scatter(values, "tensor", scatter_dimension=0, tiled=True)


def masked_scores(queries, keys, key_valid):
    scores = jnp.einsum(
        "qhd,khd->hqk", queries, keys, preferred_element_type=jnp.float32
    ) * HEAD_DIM ** (-0.5)
    return jnp.where(key_valid[None, None, :], scores, NEG_LARGE)


def attend_slot(items):
    queries, keys, values, key_valid = items
    scores = masked_scores(queries, keys, key_valid)
    top = jnp.max(scores, axis=2, keepdims=True)
    total = jnp.sum(jnp.exp(scores - top), axis=2, keepdims=True)
    logsum = top + jnp.log(total)
    probs = jnp.exp(scores - logsum).astype(jnp.bfloat16)
    mixed = jnp.einsum("hqk,khd->qhd", probs, values, preferred_element_type=jnp.float32).astype(
        jnp.bfloat16
    )
    return (mixed, logsum[:, :, 0])


def attend_back(items):
    queries, keys, values, key_valid, logsum, mixed, grad_mixed = items
    scores = masked_scores(queries, keys, key_valid)
    probs = jnp.exp(scores - logsum[:, :, None])
    rounded = probs.astype(jnp.bfloat16)
    grad_values = jnp.einsum(
        "hqk,qhd->khd", rounded, grad_mixed, preferred_element_type=jnp.float32
    )
    grad_probs = jnp.einsum("qhd,khd->hqk", grad_mixed, values, preferred_element_type=jnp.float32)
    delta = jnp.sum(grad_mixed.astype(jnp.float32) * mixed.astype(jnp.float32), axis=2).T
    grad_scores = (probs * (grad_probs - delta[:, :, None]) * HEAD_DIM ** (-0.5)).astype(
        jnp.bfloat16
    )
    grad_queries = jnp.einsum("hqk,khd->qhd", grad_scores, keys, preferred_element_type=jnp.float32)
    grad_keys = jnp.einsum("hqk,qhd->khd", grad_scores, queries, preferred_element_type=jnp.float32)
    return (grad_queries, grad_keys, grad_values)


def per_device(
    tokens,
    cotangent,
    image_group,
    first_norm_gain_param,
    first_norm_bias,
    w_qkv,
    qv_bias,
    w_out,
    out_bias,
    second_norm_gain_param,
    second_norm_bias,
    w_up,
    up_bias,
    w_down,
    down_bias,
):
    group = lax.axis_index("dp")
    member = lax.axis_index("tensor")
    members = lax.axis_size("tensor")
    local_rows = tokens.shape[0]
    group_rows = local_rows * members
    slot_count = group_rows // SEQ_PAD
    head_cols = w_out.shape[0]
    heads_here = head_cols // HEAD_DIM
    hidden_here = w_up.shape[1]
    gathered = (
        lax.all_gather(first_norm_gain_param, ("dp", "tensor"), axis=0, tiled=True),
        lax.all_gather(first_norm_bias, ("dp", "tensor"), axis=0, tiled=True),
        lax.all_gather(qv_bias, ("dp", "tensor"), axis=0, tiled=True),
        lax.all_gather(out_bias, ("dp", "tensor"), axis=0, tiled=True),
        lax.all_gather(second_norm_gain_param, ("dp", "tensor"), axis=0, tiled=True),
        lax.all_gather(second_norm_bias, ("dp", "tensor"), axis=0, tiled=True),
        lax.all_gather(up_bias, ("dp", "tensor"), axis=0, tiled=True),
        lax.all_gather(down_bias, ("dp", "tensor"), axis=0, tiled=True),
    )
    (
        first_norm_gain,
        first_norm_shift,
        qv_full,
        out_shift,
        second_norm_gain,
        second_norm_shift,
        up_full,
        down_shift,
    ) = gathered
    qkv_weight, out_weight = (
        lax.all_gather(w_qkv, "dp", axis=0, tiled=True),
        lax.all_gather(w_out, "dp", axis=1, tiled=True),
    )
    up_weight, down_weight = (
        lax.all_gather(w_up, "dp", axis=0, tiled=True),
        lax.all_gather(w_down, "dp", axis=1, tiled=True),
    )
    occupied = jnp.sum((image_group == group).astype(jnp.int32))
    positions = jnp.arange(group_rows, dtype=jnp.int32)
    key_valid = ((positions % SEQ_PAD < SEQ) & (positions // SEQ_PAD < occupied)).reshape(
        slot_count, SEQ_PAD
    )
    local_pos = member * local_rows + jnp.arange(local_rows, dtype=jnp.int32)
    row_valid = ((local_pos % SEQ_PAD < SEQ) & (local_pos // SEQ_PAD < occupied)).astype(
        jnp.float32
    )[:, None]
    qv_local = lax.dynamic_slice_in_dim(qv_full, member * 2 * head_cols, 2 * head_cols).reshape(
        2, heads_here, HEAD_DIM
    )
    up_local = lax.dynamic_slice_in_dim(up_full, member * hidden_here, hidden_here)
    layer_inputs = tokens.astype(jnp.float32)
    first_normed_rows, first_standardized, first_inverse_deviation = apply_layer_norm(
        layer_inputs, first_norm_gain, first_norm_shift
    )
    normed_full = gather_rows(first_normed_rows.astype(jnp.bfloat16))
    projected = jnp.dot(normed_full, qkv_weight, preferred_element_type=jnp.float32).reshape(
        group_rows, 3, heads_here, HEAD_DIM
    )
    queries = (projected[:, 0] + qv_local[0]).astype(jnp.bfloat16)
    keys = projected[:, 1].astype(jnp.bfloat16)
    values = (projected[:, 2] + qv_local[1]).astype(jnp.bfloat16)
    shaped = (
        queries.reshape(slot_count, SEQ_PAD, heads_here, HEAD_DIM),
        keys.reshape(slot_count, SEQ_PAD, heads_here, HEAD_DIM),
        values.reshape(slot_count, SEQ_PAD, heads_here, HEAD_DIM),
        key_valid,
    )
    mixed, logsum = lax.map(attend_slot, shaped)
    mixed_rows = mixed.reshape(group_rows, head_cols)
    attn_local = scatter_rows(jnp.dot(mixed_rows, out_weight, preferred_element_type=jnp.float32))
    residual_stream = layer_inputs + attn_local + out_shift
    second_normed_rows, second_standardized, second_inverse_deviation = apply_layer_norm(
        residual_stream, second_norm_gain, second_norm_shift
    )
    normed_two_full = gather_rows(second_normed_rows.astype(jnp.bfloat16))
    hidden = jnp.dot(normed_two_full, up_weight, preferred_element_type=jnp.float32) + up_local
    activated = gelu_value(hidden).astype(jnp.bfloat16)
    mlp_local = scatter_rows(jnp.dot(activated, down_weight, preferred_element_type=jnp.float32))
    output = (row_valid * (residual_stream + mlp_local + down_shift)).astype(jnp.bfloat16)
    output_gradient = row_valid * cotangent
    grad_out_full = gather_rows(output_gradient.astype(jnp.bfloat16))
    down_term = left_product(activated, grad_out_full)
    hidden_gradient = right_product(grad_out_full, down_weight) * gelu_slope(hidden)
    grad_hidden_b = hidden_gradient.astype(jnp.bfloat16)
    up_term = left_product(normed_two_full, grad_hidden_b)
    second_normed_gradient = scatter_rows(right_product(grad_hidden_b, up_weight))
    residual_gradient = output_gradient + layer_norm_backward(
        second_normed_gradient, second_standardized, second_inverse_deviation, second_norm_gain
    )
    grad_resid_full = gather_rows(residual_gradient.astype(jnp.bfloat16))
    out_term = left_product(mixed_rows, grad_resid_full)
    grad_mixed = right_product(grad_resid_full, out_weight).astype(jnp.bfloat16)
    back_items = shaped + (
        logsum,
        mixed,
        grad_mixed.reshape(slot_count, SEQ_PAD, heads_here, HEAD_DIM),
    )
    grad_queries, grad_keys, grad_values = lax.map(attend_back, back_items)
    grad_queries = grad_queries.reshape(group_rows, heads_here, HEAD_DIM)
    grad_keys = grad_keys.reshape(group_rows, heads_here, HEAD_DIM)
    grad_values = grad_values.reshape(group_rows, heads_here, HEAD_DIM)
    grad_projected = (
        jnp.stack([grad_queries, grad_keys, grad_values], axis=1)
        .reshape(group_rows, 3 * head_cols)
        .astype(jnp.bfloat16)
    )
    qkv_term = left_product(normed_full, grad_projected)
    (
        query_key_value_gradient,
        output_projection_gradient,
        up_projection_gradient,
        down_projection_gradient,
    ) = (
        lax.psum_scatter(qkv_term, "dp", scatter_dimension=0, tiled=True),
        lax.psum_scatter(out_term, "dp", scatter_dimension=1, tiled=True),
        lax.psum_scatter(up_term, "dp", scatter_dimension=0, tiled=True),
        lax.psum_scatter(down_term, "dp", scatter_dimension=1, tiled=True),
    )
    first_normed_gradient = scatter_rows(right_product(grad_projected, qkv_weight))
    layer_input_gradient = residual_gradient + layer_norm_backward(
        first_normed_gradient, first_standardized, first_inverse_deviation, first_norm_gain
    )
    qv_piece = jnp.concatenate(
        [
            jnp.sum(grad_queries, axis=0).reshape(head_cols),
            jnp.sum(grad_values, axis=0).reshape(head_cols),
        ]
    )
    qv_term = lax.dynamic_update_slice_in_dim(
        jnp.zeros((2 * D,), jnp.float32), qv_piece, member * 2 * head_cols, 0
    )
    up_bias_term = lax.dynamic_update_slice_in_dim(
        jnp.zeros((FF,), jnp.float32), jnp.sum(hidden_gradient, axis=0), member * hidden_here, 0
    )
    vector_terms = (
        jnp.sum(first_normed_gradient * first_standardized, axis=0),
        jnp.sum(first_normed_gradient, axis=0),
        qv_term,
        jnp.sum(residual_gradient, axis=0),
        jnp.sum(second_normed_gradient * second_standardized, axis=0),
        jnp.sum(second_normed_gradient, axis=0),
        up_bias_term,
        jnp.sum(output_gradient, axis=0),
    )
    (
        gain_one_grad,
        shift_one_grad,
        query_value_bias_gradient,
        out_shift_grad,
        gain_two_grad,
        shift_two_grad,
        up_shift_grad,
        down_shift_grad,
    ) = (
        lax.psum_scatter(vector_terms[0], ("dp", "tensor"), scatter_dimension=0, tiled=True),
        lax.psum_scatter(vector_terms[1], ("dp", "tensor"), scatter_dimension=0, tiled=True),
        lax.psum_scatter(vector_terms[2], ("dp", "tensor"), scatter_dimension=0, tiled=True),
        lax.psum_scatter(vector_terms[3], ("dp", "tensor"), scatter_dimension=0, tiled=True),
        lax.psum_scatter(vector_terms[4], ("dp", "tensor"), scatter_dimension=0, tiled=True),
        lax.psum_scatter(vector_terms[5], ("dp", "tensor"), scatter_dimension=0, tiled=True),
        lax.psum_scatter(vector_terms[6], ("dp", "tensor"), scatter_dimension=0, tiled=True),
        lax.psum_scatter(vector_terms[7], ("dp", "tensor"), scatter_dimension=0, tiled=True),
    )
    return (
        output,
        layer_input_gradient,
        gain_one_grad,
        shift_one_grad,
        query_key_value_gradient,
        query_value_bias_gradient,
        output_projection_gradient,
        out_shift_grad,
        gain_two_grad,
        shift_two_grad,
        up_projection_gradient,
        up_shift_grad,
        down_projection_gradient,
        down_shift_grad,
    )


def solution(mesh):
    placed = (
        P(("dp", "tensor"), None),
        P(("dp", "tensor"), None),
        P(),
        P(("dp", "tensor")),
        P(("dp", "tensor")),
        P("dp", "tensor"),
        P(("dp", "tensor")),
        P("tensor", "dp"),
        P(("dp", "tensor")),
        P(("dp", "tensor")),
        P(("dp", "tensor")),
        P("dp", "tensor"),
        P(("dp", "tensor")),
        P("tensor", "dp"),
        P(("dp", "tensor")),
    )
    return jax.shard_map(
        per_device,
        mesh=mesh,
        in_specs=placed,
        out_specs=(
            P(("dp", "tensor"), None),
            P(("dp", "tensor"), None),
            P(("dp", "tensor")),
            P(("dp", "tensor")),
            P("dp", "tensor"),
            P(("dp", "tensor")),
            P("tensor", "dp"),
            P(("dp", "tensor")),
            P(("dp", "tensor")),
            P(("dp", "tensor")),
            P("dp", "tensor"),
            P(("dp", "tensor")),
            P("tensor", "dp"),
            P(("dp", "tensor")),
        ),
        check_vma=False,
    )
```

profile of v0, /device:TPU:0, one launch (start us, length us, event | category | flops | bytes accessed | tf_op | source)
XLA Modules:
  0.0 735.2 jit_solution(795270520085689849)
XLA Ops:
  14.6 42.4 %all-reduce.16 = (f32[1024]{0:T(1024)S(1)}, f32[1024]{0:T(1024)S(1)}, f32[2048]{0:T(1024)S(1)}, f32[1024]{0:T(1024)S(1)}, f32[1024]{0:T(1024)S(1)}, /*index=5*/f32[1024]{0:T(1024)S(1)}) all-reduce(f32[1024]{0:T(1024)S(1)} %dynamic-update-slice.1, f32[1024]{0:T(1024)S(1)} %dynamic-update-slice, ...), channel_id=1, replica_groups=mesh['dp'=8,'tensor'=4] {'dp','tensor'}, use_global_device_ids=true, to_apply=%add.1 | all-reduce | flops 7168 | bytes 57344
  57.0 2.0 fusion.14
  62.0 11.7 %all_gather.53 = bf16[256,1024]{1,0:T(8,128)(2,1)} all-gather(bf16[256,128]{1,0:T(8,128)(2,1)} %param.22), channel_id=1, replica_groups=mesh['dp'=8,'tensor'=4] {'dp'}, dimensions={1}, use_global_device_ids=true | all-gather | bytes 589824 | tf_op jit(solution)/shard_map/all_gather | solution.py:158
  73.7 17.8 %all-gather.9.cloned.1.call-done = bf16[640,1024]{1,0:T(8,128)(2,1)} async-done(((bf16[160,1024]{1,0:T(8,128)(2,1)}), bf16[640,1024]{1,0:T(8,128)(2,1)}) %all-gather.9.cloned.1.call-update) | async-done | bytes 1310736 | tf_op jit(solution)/shard_map/all_gather | solution.py:65
  91.5 26.6 %all-gather.11.cloned.1.call-done = bf16[1024,768]{1,0:T(8,128)(2,1)} async-done(((bf16[128,768]{1,0:T(8,128)(2,1)}), bf16[1024,768]{1,0:T(8,128)(2,1)}) %all-gather.11.cloned.1.call-update) | async-done | bytes 1572880 | tf_op jit(solution)/shard_map/all_gather | solution.py:157
  118.0 3.3 fusion.52
  128.8 2.1 fusion.53
  131.5 51.8 %reduce-scatter.9.cloned.1.call-done = f32[160,1024]{1,0:T(8,128)} async-done(((f32[640,1024]{1,0:T(8,128)}), f32[160,1024]{1,0:T(8,128)}) %reduce-scatter.9.cloned.1.call-update) | async-done | bytes 655376 | tf_op jit(solution)/shard_map/reduce_scatter | solution.py:69
  187.1 1.9 multiply_convert_fusion.3
  189.9 67.6 %all-gather = f32[32,1,128]{2,1,0:T(1,128)S(1)} all-gather(f32[1,1,128]{2,1,0:T(1,128)S(1)} %bitcast.93), channel_id=1, replica_groups=mesh['dp'=8,'tensor'=4] {'dp','tensor'}, dimensions={0}, use_global_device_ids=true | all-gather | bytes 16896 | tf_op jit(solution)/shard_map/all_gather | solution.py:143
  257.5 5.7 multiply_convert_fusion.1
  263.2 17.5 %all-gather.19.cloned.1.call-done = bf16[640,1024]{1,0:T(8,128)(2,1)} async-done(((bf16[160,1024]{1,0:T(8,128)(2,1)}), bf16[640,1024]{1,0:T(8,128)(2,1)}) %all-gather.19.cloned.1.call-update) | async-done | bytes 1310736 | tf_op jit(solution)/shard_map/all_gather | solution.py:65
  280.7 29.1 %all-gather.17.cloned.1.call-done = bf16[1024,1024]{1,0:T(8,128)(2,1)} async-done(((bf16[1024,128]{1,0:T(8,128)(2,1)}), bf16[1024,1024]{1,0:T(8,128)(2,1)}) %all-gather.17.cloned.1.call-update) | async-done | bytes 2097168 | tf_op jit(solution)/shard_map/all_gather | solution.py:162
  309.9 5.3 fusion.49
  316.2 3.1 fusion.28
  319.4 52.4 %reduce-scatter.13.cloned.1.call-done = f32[160,1024]{1,0:T(8,128)} async-done(((f32[640,1024]{1,0:T(8,128)}), f32[160,1024]{1,0:T(8,128)}) %reduce-scatter.13.cloned.1.call-update) | async-done | bytes 655376 | tf_op jit(solution)/shard_map/reduce_scatter | solution.py:69
  377.0 32.2 %all-gather.21.cloned.1.call-done = bf16[640,1024]{1,0:T(8,128)(2,1)} async-done(((bf16[160,1024]{1,0:T(8,128)(2,1)}), bf16[640,1024]{1,0:T(8,128)(2,1)}) %all-gather.21.cloned.1.call-update) | async-done | bytes 1310736 | tf_op jit(solution)/shard_map/all_gather | solution.py:65
  409.2 2.2 multiply_reduce_fusion.1
  412.9 4.8 multiply_convert_fusion
  420.3 2.8 fusion.55
  424.4 4.6 fusion.54
  430.3 5.1 fusion.58
  436.8 5.1 fusion.26
  445.0 4.5 fusion.56
  450.8 23.8 %reduce-scatter.15.cloned.1.call-done = f32[160,1024]{1,0:T(8,128)} async-done(((f32[640,1024]{1,0:T(8,128)}), f32[160,1024]{1,0:T(8,128)}) %reduce-scatter.15.cloned.1.call-update) | async-done | bytes 655376 | tf_op jit(solution)/shard_map/reduce_scatter | solution.py:69
  476.2 43.9 %all-reduce.15 = (f32[1024]{0:T(1024)S(1)}, f32[1024]{0:T(1024)S(1)}, f32[1024]{0:T(1024)S(1)}, f32[2048]{0:T(1024)S(1)}, f32[1024]{0:T(1024)S(1)}, /*index=5*/f...) all-reduce(f32[1024]{0:T(1024)S(1)} %dynamic-update-slice.6, ...), channel_id=1, replica_groups=mesh['dp'=8,'tensor'=4] {'dp','tensor'}, use_global_device_ids=true, to_apply=%add.6 | all-reduce | flops 13312 | bytes 106496
  524.8 4.9 reduce-scatter.11.cloned.1.call-done
  529.7 1.9 multiply_convert_fusion.2
  532.7 51.3 %reduce-scatter.23.cloned.1.call-done = f32[1024,128]{1,0:T(8,128)} async-done(((f32[1024,1024]{1,0:T(8,128)}), f32[1024,128]{1,0:T(8,128)}) %reduce-scatter.23.cloned.1.call-update) | async-done | bytes 524304 | tf_op jit(solution)/shard_map/reduce_scatter | solution.py:243
  584.1 55.1 %reduce-scatter.21.cloned.1.call-done = f32[128,1024]{1,0:T(8,128)} async-done(((f32[1024,1024]{1,0:T(8,128)}), f32[128,1024]{1,0:T(8,128)}) %reduce-scatter.21.cloned.1.call-update) | async-done | bytes 524304 | tf_op jit(solution)/shard_map/reduce_scatter | solution.py:242
  639.2 39.6 %reduce-scatter.19.cloned.1.call-done = f32[256,128]{1,0:T(8,128)} async-done(((f32[256,1024]{1,0:T(8,128)}), f32[256,128]{1,0:T(8,128)}) %reduce-scatter.19.cloned.1.call-update) | async-done | bytes 131088 | tf_op jit(solution)/shard_map/reduce_scatter | solution.py:241
  678.8 49.9 %reduce-scatter.17.cloned.1.call-done = f32[128,768]{1,0:T(8,128)} async-done(((f32[1024,768]{1,0:T(8,128)}), f32[128,768]{1,0:T(8,128)}) %reduce-scatter.17.cloned.1.call-update) | async-done | bytes 393232 | tf_op jit(solution)/shard_map/reduce_scatter | solution.py:240
  (138 shorter events, 49.0 us)
Async XLA Ops:
  7.2 84.3 %all-gather.9.cloned.1.call-start = ((), (), s32[]{:S(2)}) async-start(), calls=%async_computation.8 | async-start | bytes 1638400 | tf_op jit(solution)/shard_map/all_gather | solution.py:65
  59.0 59.1 %all-gather.11.cloned.1.call-start = ((), (), s32[]{:S(2)}) async-start(), calls=%async_computation.9 | async-start | bytes 1769472 | tf_op jit(solution)/shard_map/all_gather | solution.py:157
  59.7 123.6 %reduce-scatter.9.cloned.1.call-start = ((), (), s32[]{:S(2)}) async-start(), calls=%async_computation.10 | async-start | bytes 3276800 | tf_op jit(solution)/shard_map/reduce_scatter | solution.py:69
  121.3 6.0 copy-start.6
  123.1 2.7 copy-start
  127.3 1.5 copy-start.11
  130.9 126.6 %all-gather.15.cloned.1.call-start = ((), (), s32[]{:S(2)}) async-start(), calls=%async_computation.12 | async-start | bytes 2359296 | tf_op jit(solution)/shard_map/all_gather | solution.py:161
  131.5 58.4 %copy-start.13 = (f32[128]{0:T(128)S(1)}, f32[128]{0:T(128)}, u32[]{:S(2)}) copy-start(f32[128]{0:T(128)} %param.27) | copy-start | bytes 1540
  131.5 126.0 %all-gather.13.cloned.1.call-start = ((), (), s32[]{:S(2)}) async-start(), calls=%async_computation.11 | async-start | bytes 1638400 | tf_op jit(solution)/shard_map/all_gather | solution.py:65
  186.4 94.3 %all-gather.19.cloned.1.call-start = ((), (), s32[]{:S(2)}) async-start(), calls=%async_computation.15 | async-start | bytes 1638400 | tf_op jit(solution)/shard_map/all_gather | solution.py:65
  189.1 120.8 %all-gather.17.cloned.1.call-start = ((), (), s32[]{:S(2)}) async-start(), calls=%async_computation.13 | async-start | bytes 2359296 | tf_op jit(solution)/shard_map/all_gather | solution.py:162
  189.8 181.9 %reduce-scatter.13.cloned.1.call-start = ((), (), s32[]{:S(2)}) async-start(), calls=%async_computation.16 | async-start | bytes 3276800 | tf_op jit(solution)/shard_map/reduce_scatter | solution.py:69
  309.9 6.3 copy-start.14
  315.1 1.1 copy-start.19
  319.3 89.8 %all-gather.21.cloned.1.call-start = ((), (), s32[]{:S(2)}) async-start(), calls=%async_computation.17 | async-start | bytes 1638400 | tf_op jit(solution)/shard_map/all_gather | solution.py:65
  376.9 97.7 %reduce-scatter.15.cloned.1.call-start = ((), (), s32[]{:S(2)}) async-start(), calls=%async_computation.18 | async-start | bytes 3276800 | tf_op jit(solution)/shard_map/reduce_scatter | solution.py:69
  411.3 1.5 copy-start.7
  418.9 1.4 copy-start.15
  423.1 1.3 copy-start.20
  423.1 106.6 %reduce-scatter.11.cloned.1.call-start = ((), (), s32[]{:S(2)}) async-start(), calls=%async_computation.14 | async-start | bytes 3276800 | tf_op jit(solution)/shard_map/reduce_scatter | solution.py:69
  429.0 1.3 copy-start.17
  429.1 155.0 %reduce-scatter.23.cloned.1.call-start = ((), (), s32[]{:S(2)}) async-start(), calls=%async_computation.22 | async-start | bytes 4718592 | tf_op jit(solution)/shard_map/reduce_scatter | solution.py:243
  435.4 1.3 copy-start.16
  435.4 203.7 %reduce-scatter.21.cloned.1.call-start = ((), (), s32[]{:S(2)}) async-start(), calls=%async_computation.21 | async-start | bytes 4718592 | tf_op jit(solution)/shard_map/reduce_scatter | solution.py:242
  441.9 1.0 copy-start.9
  441.9 1.5 copy-start.12
  441.9 236.9 %reduce-scatter.19.cloned.1.call-start = ((), (), s32[]{:S(2)}) async-start(), calls=%async_computation.20 | async-start | bytes 1179648 | tf_op jit(solution)/shard_map/reduce_scatter | solution.py:241
  444.9 283.8 %reduce-scatter.17.cloned.1.call-start = ((), (), s32[]{:S(2)}) async-start(), calls=%async_computation.19 | async-start | bytes 3538944 | tf_op jit(solution)/shard_map/reduce_scatter | solution.py:240
  449.5 25.2 %copy-start.3 = (bf16[160,1024]{1,0:T(8,128)(2,1)S(1)}, bf16[160,1024]{1,0:T(8,128)(2,1)}, u32[]{:S(2)}) copy-start(bf16[160,1024]{1,0:T(8,128)(2,1)} %param.15) | copy-start | bytes 983044
  449.5 80.2 %copy-start.2 = (f32[160,1024]{1,0:T(8,128)S(1)}, f32[160,1024]{1,0:T(8,128)}, u32[]{:S(2)}) copy-start(f32[160,1024]{1,0:T(8,128)} %copy-done.1) | copy-start | bytes 1966084
  449.5 82.2 %copy-start.5 = (f32[160,1024]{1,0:T(8,128)S(1)}, f32[160,1024]{1,0:T(8,128)}, u32[]{:S(2)}) copy-start(f32[160,1024]{1,0:T(8,128)} %copy-done.4) | copy-start | bytes 1966084
  474.6 57.0 %copy-start.10 = (f32[160,1024]{1,0:T(8,128)S(1)}, f32[160,1024]{1,0:T(8,128)}, u32[]{:S(2)}) copy-start(f32[160,1024]{1,0:T(8,128)} %reduce-scatter.15.cloned.1.call-done) | copy-start | bytes 1966084
  (4 other events, 3.1 us)
Sparse Core Ops, SparseCore 0:
  59.1 32.3 all-gather.8
  93.3 24.6 all-gather.10
  131.0 52.2 reduce-scatter.8
  185.1 27.3 all-gather.14
  214.4 32.6 all-gather.12
  249.1 31.6 all-gather.18
  282.6 27.1 all-gather.16
  319.5 52.2 reduce-scatter.12
  377.1 32.0 all-gather.20
  423.3 51.3 reduce-scatter.14
  477.0 52.7 reduce-scatter.10
  533.5 50.5 reduce-scatter.22
  588.0 51.1 reduce-scatter.20
  642.8 35.9 reduce-scatter.18
  682.6 46.0 reduce-scatter.16
where the time goes:
time: 736 us; the launch traced here: 735 us
  waiting for transfers between devices  454 us (62%)
  blocking collectives  166 us (23%)
  matrix products  55.6 us (8%)
  other arithmetic  23.3 us (3%)
  local copies, waits for them, and re-layouts  21.4 us (3%)
  between operations  14.3 us (2%)
    reduce_scatter x4, waiting for transfers between devices, scatter_rows(): return lax.psum_scatter(values, 'tensor', scatter_dimension=0, tiled=True)  133 us
    unnamed x2, blocking collectives  86.3 us
    all_gather x1, blocking collectives, per_device(): lax.all_gather(up_bias, ('dp', 'tensor'), axis=0, tiled=True)  67.6 us
    all_gather x4, waiting for transfers between devices, gather_rows(): return lax.all_gather(values, 'tensor', axis=0, tiled=True)  67.5 us
    reduce_scatter x1, waiting for transfers between devices, per_device(): lax.psum_scatter(up_term, 'dp', scatter_dimension=0, tiled=True)  55.1 us
    reduce_scatter x1, waiting for transfers between devices, per_device(): lax.psum_scatter(down_term, 'dp', scatter_dimension=1, tiled=True)  51.3 us
    reduce_scatter x1, waiting for transfers between devices, per_device(): lax.psum_scatter(qkv_term, 'dp', scatter_dimension=0, tiled=True)  49.9 us
    reduce_scatter x1, waiting for transfers between devices, per_device(): lax.psum_scatter(out_term, 'dp', scatter_dimension=1, tiled=True)  39.6 us
  transfers between devices with their start and end apart: 15, of which 13 were waited for; matrix products, arithmetic and copies ran while one was open for 6% of the time, Pallas kernels for 0%

commit v1 on v0

--- a/solution.py
+++ b/solution.py
@@ -66,7 +66,29 @@
 
 
 def scatter_rows(values):
-    return lax.psum_scatter(values, "tensor", scatter_dimension=0, tiled=True)
+    return lax.psum_scatter(
+        values.astype(jnp.bfloat16), "tensor", scatter_dimension=0, tiled=True
+    ).astype(jnp.float32)
+
+
+def gather_weights(w_qkv, w_out, w_up, w_down):
+    return (
+        lax.all_gather(w_qkv, "dp", axis=0, tiled=True),
+        lax.all_gather(w_out, "dp", axis=1, tiled=True),
+        lax.all_gather(w_up, "dp", axis=0, tiled=True),
+        lax.all_gather(w_down, "dp", axis=1, tiled=True),
+    )
+
+
+def reduce_grads(row_split, column_split):
+    return (
+        lax.psum_scatter(
+            row_split.astype(jnp.bfloat16), "dp", scatter_dimension=0, tiled=True
+        ).astype(jnp.float32),
+        lax.psum_scatter(
+            column_split.astype(jnp.bfloat16), "dp", scatter_dimension=1, tiled=True
+        ).astype(jnp.float32),
+    )
 
 
 def masked_scores(queries, keys, key_valid):
@@ -105,6 +127,12 @@
     grad_queries = jnp.einsum("hqk,khd->qhd", grad_scores, keys, preferred_element_type=jnp.float32)
     grad_keys = jnp.einsum("hqk,qhd->khd", grad_scores, queries, preferred_element_type=jnp.float32)
     return (grad_queries, grad_keys, grad_values)
+
+
+def per_slot(attend, items):
+    if items[0].shape[0] > 1:
+        return lax.map(attend, items)
+    return tuple(result[None] for result in attend(tuple(item[0] for item in items)))
 
 
 def per_device(
@@ -133,16 +161,21 @@
     head_cols = w_out.shape[0]
     heads_here = head_cols // HEAD_DIM
     hidden_here = w_up.shape[1]
-    gathered = (
-        lax.all_gather(first_norm_gain_param, ("dp", "tensor"), axis=0, tiled=True),
-        lax.all_gather(first_norm_bias, ("dp", "tensor"), axis=0, tiled=True),
-        lax.all_gather(qv_bias, ("dp", "tensor"), axis=0, tiled=True),
-        lax.all_gather(out_bias, ("dp", "tensor"), axis=0, tiled=True),
-        lax.all_gather(second_norm_gain_param, ("dp", "tensor"), axis=0, tiled=True),
-        lax.all_gather(second_norm_bias, ("dp", "tensor"), axis=0, tiled=True),
-        lax.all_gather(up_bias, ("dp", "tensor"), axis=0, tiled=True),
-        lax.all_gather(down_bias, ("dp", "tensor"), axis=0, tiled=True),
-    )
+    tokens_full = gather_rows(tokens)
+    qkv_weight, out_weight, up_weight, down_weight = gather_weights(w_qkv, w_out, w_up, w_down)
+    pieces = (
+        first_norm_gain_param,
+        first_norm_bias,
+        qv_bias,
+        out_bias,
+        second_norm_gain_param,
+        second_norm_bias,
+        up_bias,
+        down_bias,
+    )
+    widths = [piece.shape[0] for piece in pieces]
+    packed = lax.all_gather(jnp.concatenate(pieces), ("dp", "tensor"), axis=0)
+    ends = [sum(widths[: n + 1]) for n in range(len(widths))]
     (
         first_norm_gain,
         first_norm_shift,
@@ -152,15 +185,7 @@
         second_norm_shift,
         up_full,
         down_shift,
-    ) = gathered
-    qkv_weight, out_weight = (
-        lax.all_gather(w_qkv, "dp", axis=0, tiled=True),
-        lax.all_gather(w_out, "dp", axis=1, tiled=True),
-    )
-    up_weight, down_weight = (
-        lax.all_gather(w_up, "dp", axis=0, tiled=True),
-        lax.all_gather(w_down, "dp", axis=1, tiled=True),
-    )
+    ) = [packed[:, end - width : end].reshape(-1) for width, end in zip(widths, ends)]
     occupied = jnp.sum((image_group == group).astype(jnp.int32))
     positions = jnp.arange(group_rows, dtype=jnp.int32)
     key_valid = ((positions % SEQ_PAD < SEQ) & (positions // SEQ_PAD < occupied)).reshape(
@@ -175,10 +200,15 @@
     )
     up_local = lax.dynamic_slice_in_dim(up_full, member * hidden_here, hidden_here)
     layer_inputs = tokens.astype(jnp.float32)
-    first_normed_rows, first_standardized, first_inverse_deviation = apply_layer_norm(
+    _, first_standardized, first_inverse_deviation = apply_layer_norm(
         layer_inputs, first_norm_gain, first_norm_shift
     )
-    normed_full = gather_rows(first_normed_rows.astype(jnp.bfloat16))
+    normed_rows, standardized_full, _ = apply_layer_norm(
+        tokens_full.astype(jnp.float32), first_norm_gain, first_norm_shift
+    )
+    normed_full = normed_rows.astype(jnp.bfloat16)
+    output_gradient = row_valid * cotangent
+    grad_out_full = gather_rows(output_gradient.astype(jnp.bfloat16))
     projected = jnp.dot(normed_full, qkv_weight, preferred_element_type=jnp.float32).reshape(
         group_rows, 3, heads_here, HEAD_DIM
     )
@@ -191,7 +221,7 @@
         values.reshape(slot_count, SEQ_PAD, heads_here, HEAD_DIM),
         key_valid,
     )
-    mixed, logsum = lax.map(attend_slot, shaped)
+    mixed, logsum = per_slot(attend_slot, shaped)
     mixed_rows = mixed.reshape(group_rows, head_cols)
     attn_local = scatter_rows(jnp.dot(mixed_rows, out_weight, preferred_element_type=jnp.float32))
     residual_stream = layer_inputs + attn_local + out_shift
@@ -203,12 +233,11 @@
     activated = gelu_value(hidden).astype(jnp.bfloat16)
     mlp_local = scatter_rows(jnp.dot(activated, down_weight, preferred_element_type=jnp.float32))
     output = (row_valid * (residual_stream + mlp_local + down_shift)).astype(jnp.bfloat16)
-    output_gradient = row_valid * cotangent
-    grad_out_full = gather_rows(output_gradient.astype(jnp.bfloat16))
     down_term = left_product(activated, grad_out_full)
     hidden_gradient = right_product(grad_out_full, down_weight) * gelu_slope(hidden)
     grad_hidden_b = hidden_gradient.astype(jnp.bfloat16)
     up_term = left_product(normed_two_full, grad_hidden_b)
+    up_projection_gradient, down_projection_gradient = reduce_grads(up_term, down_term)
     second_normed_gradient = scatter_rows(right_product(grad_hidden_b, up_weight))
     residual_gradient = output_gradient + layer_norm_backward(
         second_normed_gradient, second_standardized, second_inverse_deviation, second_norm_gain
@@ -221,7 +250,7 @@
         mixed,
         grad_mixed.reshape(slot_count, SEQ_PAD, heads_here, HEAD_DIM),
     )
-    grad_queries, grad_keys, grad_values = lax.map(attend_back, back_items)
+    grad_queries, grad_keys, grad_values = per_slot(attend_back, back_items)
     grad_queries = grad_queries.reshape(group_rows, heads_here, HEAD_DIM)
     grad_keys = grad_keys.reshape(group_rows, heads_here, HEAD_DIM)
     grad_values = grad_values.reshape(group_rows, heads_here, HEAD_DIM)
@@ -231,18 +260,9 @@
         .astype(jnp.bfloat16)
     )
     qkv_term = left_product(normed_full, grad_projected)
-    (
-        query_key_value_gradient,
-        output_projection_gradient,
-        up_projection_gradient,
-        down_projection_gradient,
-    ) = (
-        lax.psum_scatter(qkv_term, "dp", scatter_dimension=0, tiled=True),
-        lax.psum_scatter(out_term, "dp", scatter_dimension=1, tiled=True),
-        lax.psum_scatter(up_term, "dp", scatter_dimension=0, tiled=True),
-        lax.psum_scatter(down_term, "dp", scatter_dimension=1, tiled=True),
-    )
-    first_normed_gradient = scatter_rows(right_product(grad_projected, qkv_weight))
+    query_key_value_gradient, output_projection_gradient = reduce_grads(qkv_term, out_term)
+    first_normed_terms = right_product(grad_projected, qkv_weight)
+    first_normed_gradient = scatter_rows(first_normed_terms)
     layer_input_gradient = residual_gradient + layer_norm_backward(
         first_normed_gradient, first_standardized, first_inverse_deviation, first_norm_gain
     )
@@ -259,14 +279,20 @@
         jnp.zeros((FF,), jnp.float32), jnp.sum(hidden_gradient, axis=0), member * hidden_here, 0
     )
     vector_terms = (
-        jnp.sum(first_normed_gradient * first_standardized, axis=0),
-        jnp.sum(first_normed_gradient, axis=0),
+        jnp.sum(first_normed_terms * standardized_full, axis=0),
+        jnp.sum(first_normed_terms, axis=0),
         qv_term,
         jnp.sum(residual_gradient, axis=0),
         jnp.sum(second_normed_gradient * second_standardized, axis=0),
         jnp.sum(second_normed_gradient, axis=0),
         up_bias_term,
         jnp.sum(output_gradient, axis=0),
+    )
+    packed_terms = jnp.concatenate(
+        [term.reshape(-1, width) for term, width in zip(vector_terms, widths)], axis=1
+    )
+    packed_grad = lax.psum_scatter(
+        packed_terms, ("dp", "tensor"), scatter_dimension=0, tiled=False
     )
     (
         gain_one_grad,
@@ -277,16 +303,7 @@
         shift_two_grad,
         up_shift_grad,
         down_shift_grad,
-    ) = (
-        lax.psum_scatter(vector_terms[0], ("dp", "tensor"), scatter_dimension=0, tiled=True),
-        lax.psum_scatter(vector_terms[1], ("dp", "tensor"), scatter_dimension=0, tiled=True),
-        lax.psum_scatter(vector_terms[2], ("dp", "tensor"), scatter_dimension=0, tiled=True),
-        lax.psum_scatter(vector_terms[3], ("dp", "tensor"), scatter_dimension=0, tiled=True),
-        lax.psum_scatter(vector_terms[4], ("dp", "tensor"), scatter_dimension=0, tiled=True),
-        lax.psum_scatter(vector_terms[5], ("dp", "tensor"), scatter_dimension=0, tiled=True),
-        lax.psum_scatter(vector_terms[6], ("dp", "tensor"), scatter_dimension=0, tiled=True),
-        lax.psum_scatter(vector_terms[7], ("dp", "tensor"), scatter_dimension=0, tiled=True),
-    )
+    ) = [packed_grad[end - width : end] for width, end in zip(widths, ends)]
     return (
         output,
         layer_input_gradient,

time: 736 us -> 584 us (0.79)
  waiting for transfers between devices: 454 us -> 340 us
  blocking collectives: 166 us -> 122 us
    reduce_scatter x8 -> x6, waiting for transfers between devices: 329 us -> 193 us  [the longest x4 117 us: scatter_rows(): lax.psum_scatter(values.astype(jnp.bfloat16), 'tensor', scatter_dimension...]
    unnamed x2 -> x1, blocking collectives: 86.3 us -> 39.7 us
    unnamed x15 -> x17, waiting for transfers between devices: 2.11 us -> 18.4 us
    all_gather x4, waiting for transfers between devices: 67.5 us -> 79.6 us  [gather_rows(): return lax.all_gather(values, 'tensor', axis=0, tiled=True)]
    unnamed x65 -> x30, local copies, waits for them, and re-layouts: 20.8 us -> 12.1 us
  transfers between devices with their start and end apart: 15 -> 15, of which waited for: 13 -> 12; matrix products, arithmetic and copies ran while one was open for 6% -> 13% of each run, Pallas kernels for 0% -> 0%
where the time goes in v1:
time: 584 us; the launch traced here: 583 us
  waiting for transfers between devices  340 us (58%)
  blocking collectives  122 us (21%)
  matrix products  59.9 us (10%)
  other arithmetic  29.4 us (5%)
  local copies, waits for them, and re-layouts  16.7 us (3%)
  between operations  14.3 us (2%)
    reduce_scatter x4, waiting for transfers between devices, scatter_rows(): lax.psum_scatter(values.astype(jnp.bfloat16), 'tensor', scatter_dimension...  117 us
    all_gather x4, waiting for transfers between devices, gather_rows(): return lax.all_gather(values, 'tensor', axis=0, tiled=True)  79.6 us
    reduce_scatter x2, waiting for transfers between devices, reduce_grads(): lax.psum_scatter(row_split.astype(jnp.bfloat16), 'dp', scatter_dimension=...  75.6 us
    all_gather x1, blocking collectives, per_device(): packed = lax.all_gather(jnp.concatenate(pieces), ('dp', 'tensor'), axis=0)  71.2 us
    unnamed x1, blocking collectives  39.7 us
    all_gather x1, waiting for transfers between devices, gather_weights(): lax.all_gather(w_down, 'dp', axis=1, tiled=True)  29.1 us
    all_gather x1, waiting for transfers between devices, gather_weights(): lax.all_gather(w_up, 'dp', axis=0, tiled=True)  19.9 us
    unnamed x17, waiting for transfers between devices  18.4 us
  transfers between devices with their start and end apart: 15, of which 12 were waited for; matrix products, arithmetic and copies ran while one was open for 13% of the time, Pallas kernels for 0%

profile of v1, /device:TPU:0, one launch (start us, length us, event | category | flops | bytes accessed | tf_op | source)
XLA Modules:
  0.0 583.0 jit_solution(5508817746720197506)
XLA Ops:
  9.6 71.2 %all-gather.1 = f32[32,1,384]{2,1,0:T(1,128)S(1)} all-gather(f32[1,1,384]{2,1,0:T(1,128)S(1)} %reshape.218), channel_id=2, replica_groups=mesh['dp'=8,'tensor'=4] {'dp','tensor'}, dimensions={0}, use_global_device_ids=true | all-gather | bytes 50688 | tf_op jit(solution)/shard_map/all_gather | solution.py:177
  83.4 11.1 %all_gather.34 = bf16[256,1024]{1,0:T(8,128)(2,1)} all-gather(bf16[256,128]{1,0:T(8,128)(2,1)} %param.22), channel_id=1, replica_groups=mesh['dp'=8,'tensor'=4] {'dp'}, dimensions={1}, use_global_device_ids=true | all-gather | bytes 589824 | tf_op jit(solution)/shard_map/all_gather | solution.py:77
  98.0 3.0 fusion.55
  110.9 27.9 %reduce-scatter.13.cloned.1.call-done = bf16[160,1024]{1,0:T(8,128)(2,1)} async-done(((bf16[640,1024]{1,0:T(8,128)(2,1)}), bf16[160,1024]{1,0:T(8,128)(2,1)}) %reduce-scatter.13.cloned.1.call-update) | async-done | bytes 327696 | tf_op jit(solution)/shard_map/reduce_scatter | solution.py:69
  147.2 19.9 %all-gather.16.cloned.1.call-done = bf16[1024,1024]{1,0:T(8,128)(2,1)} async-done(((bf16[128,1024]{1,0:T(8,128)(2,1)}), bf16[1024,1024]{1,0:T(8,128)(2,1)}) %all-gather.16.cloned.1.call-update) | async-done | bytes 2097168 | tf_op jit(solution)/shard_map/all_gather | solution.py:78
  167.1 34.5 %all-gather.14.cloned.1.call-done = bf16[640,1024]{1,0:T(8,128)(2,1)} async-done(((bf16[160,1024]{1,0:T(8,128)(2,1)}), bf16[640,1024]{1,0:T(8,128)(2,1)}) %all-gather.14.cloned.1.call-update) | async-done | bytes 1310736 | tf_op jit(solution)/shard_map/all_gather | solution.py:65
  201.6 5.7 multiply_convert_fusion.1
  207.3 28.0 %all-gather.20.cloned.1.call-done = bf16[640,1024]{1,0:T(8,128)(2,1)} async-done(((bf16[160,1024]{1,0:T(8,128)(2,1)}), bf16[640,1024]{1,0:T(8,128)(2,1)}) %all-gather.20.cloned.1.call-update) | async-done | bytes 1310736 | tf_op jit(solution)/shard_map/all_gather | solution.py:65
  235.2 29.1 %all-gather.18.cloned.1.call-done = bf16[1024,1024]{1,0:T(8,128)(2,1)} async-done(((bf16[1024,128]{1,0:T(8,128)(2,1)}), bf16[1024,1024]{1,0:T(8,128)(2,1)}) %all-gather.18.cloned.1.call-update) | async-done | bytes 2097168 | tf_op jit(solution)/shard_map/all_gather | solution.py:79
  264.4 5.3 fusion.64
  270.7 2.6 convolution_convert_fusion.4
  273.4 4.7 convolution_convert_fusion.5
  278.2 26.7 %reduce-scatter.17.cloned.1.call-done = bf16[160,1024]{1,0:T(8,128)(2,1)} async-done(((bf16[640,1024]{1,0:T(8,128)(2,1)}), bf16[160,1024]{1,0:T(8,128)(2,1)}) %reduce-scatter.17.cloned.1.call-update) | async-done | bytes 327696 | tf_op jit(solution)/shard_map/reduce_scatter | solution.py:69
  306.6 30.7 %reduce-scatter.15.cloned.1.call-done = bf16[160,1024]{1,0:T(8,128)(2,1)} async-done(((bf16[640,1024]{1,0:T(8,128)(2,1)}), bf16[160,1024]{1,0:T(8,128)(2,1)}) %reduce-scatter.15.cloned.1.call-update) | async-done | bytes 327696 | tf_op jit(solution)/shard_map/reduce_scatter | solution.py:69
  337.3 2.8 fusion.58
  341.7 4.9 convolution_convert_fusion
  346.6 4.1 copy.57
  350.8 4.9 convolution_convert_fusion.1
  356.0 17.0 %all-gather.22.cloned.1.call-done = bf16[640,1024]{1,0:T(8,128)(2,1)} async-done(((bf16[160,1024]{1,0:T(8,128)(2,1)}), bf16[640,1024]{1,0:T(8,128)(2,1)}) %all-gather.22.cloned.1.call-update) | async-done | bytes 1310736 | tf_op jit(solution)/shard_map/all_gather | solution.py:65
  373.0 2.8 convolution_convert_fusion.6
  377.9 2.1 multiply_reduce_fusion
  382.0 6.2 %multiply_convert_fusion = bf16[4,640,640]{1,2,0:T(8,128)(2,1)S(1)} fusion(f32[4,640,640]{1,2,0:T(8,128)} %copy-done, f32[4,640]{1,0:T(4,128)S(1)} %bitcast.122, f32[4,640]{1,0:T(4,128)S(1)} %log_add_fusion, pred[640]{0:T(1024)(128)(4,1)S(1)} %fusion.51, bf16[640,4,64]{0,2,1:T(8,128)(2,1)S(1)} %bitcast.118, f32[640,3,4,64]{0,3,2,1:T(8,128)} %bitcast.106, ...), kind=kOutput, calls=%fused_computation | convolution fusion | flops 221511680 | bytes 10835584 | tf_op jit(solution)/shard_map/qhd,khd->hqk/dot_general | solution.py:122
  388.3 2.3 fusion.60
  390.6 2.4 fusion.14
  393.1 2.9 convolution_convert_fusion.2
  396.1 4.1 fusion.57
  400.9 15.7 %reduce-scatter.27.cloned.1.call-done = bf16[128,1024]{1,0:T(8,128)(2,1)} async-done(((bf16[1024,1024]{1,0:T(8,128)(2,1)}), bf16[128,1024]{1,0:T(8,128)(2,1)}) %reduce-scatter.27.cloned.1.call-update) | async-done | bytes 262160
  418.5 42.3 %reduce-scatter.23.cloned.1.call-done = bf16[128,1024]{1,0:T(8,128)(2,1)} async-done(((bf16[1024,1024]{1,0:T(8,128)(2,1)}), bf16[128,1024]{1,0:T(8,128)(2,1)}) %reduce-scatter.23.cloned.1.call-update) | async-done | bytes 262160 | tf_op jit(solution)/shard_map/reduce_scatter | solution.py:85
  463.2 39.7 %all-reduce = f32[32,384]{1,0:T(8,128)S(1)} all-reduce(f32[32,384]{1,0:T(8,128)S(1)} %concatenate.11), channel_id=7, replica_groups=mesh['dp'=8,'tensor'=4] {'dp','tensor'}, use_global_device_ids=true, to_apply=%region_27.28.clone | all-reduce | flops 12288 | bytes 98304
  506.3 33.3 %reduce-scatter.21.cloned.1.call-done = bf16[128,768]{1,0:T(8,128)(2,1)} async-done(((bf16[1024,768]{1,0:T(8,128)(2,1)}), bf16[128,768]{1,0:T(8,128)(2,1)}) %reduce-scatter.21.cloned.1.call-update) | async-done | bytes 196624 | tf_op jit(solution)/shard_map/reduce_scatter | solution.py:85
  541.3 31.9 %reduce-scatter.19.cloned.1.call-done = bf16[160,1024]{1,0:T(8,128)(2,1)} async-done(((bf16[640,1024]{1,0:T(8,128)(2,1)}), bf16[160,1024]{1,0:T(8,128)(2,1)}) %reduce-scatter.19.cloned.1.call-update) | async-done | bytes 327696 | tf_op jit(solution)/shard_map/reduce_scatter | solution.py:69
  574.4 2.1 fusion.25
  (129 shorter events, 47.0 us)
Async XLA Ops:
  7.2 87.3 %all-gather.10.cloned.1.call-start = ((), (), s32[]{:S(2)}) async-start(), calls=%async_computation.8 | async-start | bytes 1638400 | tf_op jit(solution)/shard_map/all_gather | solution.py:65
  7.9 90.0 %all-gather.12.cloned.1.call-start = ((), (), s32[]{:S(2)}) async-start(), calls=%async_computation.9 | async-start | bytes 1769472 | tf_op jit(solution)/shard_map/all_gather | solution.py:76
  8.7 130.1 %reduce-scatter.13.cloned.1.call-start = ((), (), s32[]{:S(2)}) async-start(), calls=%async_computation.10 | async-start | bytes 1638400 | tf_op jit(solution)/shard_map/reduce_scatter | solution.py:69
  94.4 3.5 copy-start.5
  101.0 6.0 %copy-start.4 = (f32[640,768]{0,1:T(8,128)}, f32[640,768]{0,1:T(8,128)S(1)}, u32[]{:S(2)}) copy-start(f32[640,768]{0,1:T(8,128)S(1)} %fusion.55) | copy-start | bytes 5898244
  102.7 2.7 copy-start
  107.0 1.5 copy-start.9
  107.7 0.7 copy-start.8
  110.0 57.0 %all-gather.16.cloned.1.call-start = ((), (), s32[]{:S(2)}) async-start(), calls=%async_computation.12 | async-start | bytes 2359296 | tf_op jit(solution)/shard_map/all_gather | solution.py:78
  110.6 91.0 %all-gather.14.cloned.1.call-start = ((), (), s32[]{:S(2)}) async-start(), calls=%async_computation.11 | async-start | bytes 1638400 | tf_op jit(solution)/shard_map/all_gather | solution.py:65
  143.4 91.8 %all-gather.20.cloned.1.call-start = ((), (), s32[]{:S(2)}) async-start(), calls=%async_computation.15 | async-start | bytes 1638400 | tf_op jit(solution)/shard_map/all_gather | solution.py:65
  146.1 118.3 %all-gather.18.cloned.1.call-start = ((), (), s32[]{:S(2)}) async-start(), calls=%async_computation.13 | async-start | bytes 2359296 | tf_op jit(solution)/shard_map/all_gather | solution.py:79
  146.9 158.0 %reduce-scatter.17.cloned.1.call-start = ((), (), s32[]{:S(2)}) async-start(), calls=%async_computation.16 | async-start | bytes 1638400 | tf_op jit(solution)/shard_map/reduce_scatter | solution.py:69
  264.4 6.3 %copy-start.10 = (bf16[1024,1024]{1,0:T(8,128)(2,1)S(1)}, bf16[1024,1024]{1,0:T(8,128)(2,1)}, u32[]{:S(2)}) copy-start(bf16[1024,1024]{1,0:T(8,128)(2,1)} %all-gather.16.cloned.1.call-done) | copy-start | bytes 6291460
  269.6 1.1 copy-start.11
  273.3 63.9 %reduce-scatter.15.cloned.1.call-start = ((), (), s32[]{:S(2)}) async-start(), calls=%async_computation.14 | async-start | bytes 1638400 | tf_op jit(solution)/shard_map/reduce_scatter | solution.py:69
  278.1 94.9 %all-gather.22.cloned.1.call-start = ((), (), s32[]{:S(2)}) async-start(), calls=%async_computation.17 | async-start | bytes 1638400 | tf_op jit(solution)/shard_map/all_gather | solution.py:65
  340.0 0.8 copy-start.2
  341.7 74.9 %reduce-scatter.27.cloned.1.call-start = ((), (), s32[]{:S(2)}) async-start(), calls=%async_computation.22 | async-start | bytes 2359296
  350.7 110.1 %reduce-scatter.23.cloned.1.call-start = ((), (), s32[]{:S(2)}) async-start(), calls=%async_computation.20 | async-start | bytes 2359296 | tf_op jit(solution)/shard_map/reduce_scatter | solution.py:85
  355.7 148.9 %reduce-scatter.25.cloned.1.call-start = ((), (), s32[]{:S(2)}) async-start(), calls=%async_computation.21 | async-start | bytes 589824
  388.2 151.3 %reduce-scatter.21.cloned.1.call-start = ((), (), s32[]{:S(2)}) async-start(), calls=%async_computation.19 | async-start | bytes 1769472 | tf_op jit(solution)/shard_map/reduce_scatter | solution.py:85
  390.6 2.5 copy-start.6
  393.1 3.0 copy-start.7
  396.1 177.1 %reduce-scatter.19.cloned.1.call-start = ((), (), s32[]{:S(2)}) async-start(), calls=%async_computation.18 | async-start | bytes 1638400 | tf_op jit(solution)/shard_map/reduce_scatter | solution.py:69
  400.2 172.9 %copy-start.1 = (bf16[160,1024]{1,0:T(8,128)(2,1)S(1)}, bf16[160,1024]{1,0:T(8,128)(2,1)}, u32[]{:S(2)}) copy-start(bf16[160,1024]{1,0:T(8,128)(2,1)} %param.15) | copy-start | bytes 983044
  400.2 174.1 %copy-start.3 = (f32[160,1024]{1,0:T(8,128)S(1)}, f32[160,1024]{1,0:T(8,128)}, u32[]{:S(2)}) copy-start(f32[160,1024]{1,0:T(8,128)} %copy-done.2) | copy-start | bytes 1966084
Sparse Core Ops, SparseCore 0:
  9.6 35.6 all-gather.9
  47.1 24.6 all-gather.11
  110.2 28.6 reduce-scatter.12
  140.6 26.4 all-gather.15
  169.0 32.5 all-gather.13
  203.6 31.6 all-gather.19
  237.1 27.1 all-gather.17
  273.5 31.3 reduce-scatter.16
  307.2 30.0 reduce-scatter.14
  341.8 31.1 all-gather.21
  376.3 40.2 reduce-scatter.26
  419.7 41.0 reduce-scatter.22
  463.9 34.0 reduce-scatter.24
  501.2 38.3 reduce-scatter.20
  541.7 31.3 reduce-scatter.18

commit v2 on v1

--- a/solution.py
+++ b/solution.py
@@ -1,6 +1,10 @@
+import functools
+
 import jax
 import jax.numpy as jnp
 from jax import lax
+from jax.experimental import pallas as pl
+from jax.experimental.pallas import tpu as pltpu
 from jax.sharding import PartitionSpec as P
 
 D = 1024
@@ -69,6 +73,321 @@
     return lax.psum_scatter(
         values.astype(jnp.bfloat16), "tensor", scatter_dimension=0, tiled=True
     ).astype(jnp.float32)
+
+
+MESH_ID = pl.DeviceIdType.MESH
+LANES = 128
+VEC_ROWS = 16
+
+
+def dp_peers():
+    me = lax.axis_index("dp")
+    core, along_x, along_y = me % 2, (me // 2) % 2, me // 4
+    index = []
+    for flip in range(8):
+        flip_core, flip_x, flip_y = flip % 2, (flip // 2) % 2, flip // 4
+        new_core = 1 - core if flip_core else core
+        new_x = 1 - along_x if flip_x else along_x
+        new_y = 1 - along_y if flip_y else along_y
+        index.append((new_y * 2 + new_x) * 2 + new_core)
+    return index
+
+
+def enter(tensor_size):
+    peer = dp_peers()
+    barrier = pltpu.get_barrier_semaphore()
+    for flip in (1, 2, 4):
+        pl.semaphore_signal(
+            barrier, inc=1, device_id={"dp": peer[flip]}, device_id_type=MESH_ID
+        )
+    z_me = lax.axis_index("tensor")
+    for hop in range(1, tensor_size):
+        pl.semaphore_signal(
+            barrier,
+            inc=1,
+            device_id={"tensor": lax.rem(z_me + hop, tensor_size)},
+            device_id_type=MESH_ID,
+        )
+    pl.semaphore_wait(barrier, 2 + tensor_size)
+    return peer, z_me
+
+
+def part(ref, owner, axis, half=None):
+    rows, columns = ref.shape
+    if axis == 0:
+        size = rows // 8
+        start, count = owner * size, size
+        if half is not None:
+            start, count = start + half * (size // 2), size // 2
+        return ref.at[pl.ds(pl.multiple_of(start, count), count), :]
+    start, count = 0, rows
+    if half is not None:
+        start, count = half * (rows // 2), rows // 2
+    return ref.at[
+        pl.ds(start, count), pl.ds(pl.multiple_of(owner * LANES, LANES), LANES)
+    ]
+
+
+def send(source, target, send_sem, recv_sem, device):
+    copy = pltpu.make_async_remote_copy(
+        src_ref=source,
+        dst_ref=target,
+        send_sem=send_sem,
+        recv_sem=recv_sem,
+        device_id=device,
+        device_id_type=MESH_ID,
+    )
+    copy.start()
+    return copy
+
+
+def gather_kernel(axes, tensor_size, *refs):
+    count = len(axes)
+    shards, fulls = refs[:count], refs[count : 2 * count]
+    vec_all = refs[2 * count]
+    send_sems, recv_sems, local_sems, z_send, z_recv = refs[2 * count + 1 :]
+    peer, z_me = enter(tensor_size)
+    slots = {1: 0, 2: 1, 3: 2, 4: 3, 5: 4, 6: 5, 7: 7}
+    sent = []
+    locals_ = []
+
+    def give(w, held, half, to, source=None):
+        target = part(fulls[w], peer[held], axes[w], half)
+        slot = slots[held ^ to] + (half or 0)
+        sent.append(
+            send(
+                target if source is None else source,
+                target,
+                send_sems.at[w, slots[held ^ to] + (half or 0)],
+                recv_sems.at[w, slot],
+                {"dp": peer[to]},
+            )
+        )
+
+    def take(w, held, half):
+        block = part(fulls[w], peer[held], axes[w], half)
+        pltpu.make_async_copy(block, block, recv_sems.at[w, slots[held] + (half or 0)]).wait()
+
+    for w in range(count):
+        own = pltpu.make_async_copy(
+            shards[w], part(fulls[w], peer[0], axes[w]), local_sems.at[w]
+        )
+        own.start()
+        locals_.append(own)
+        for to in (2, 4, 1):
+            give(w, 0, None, to, shards[w])
+    for w in range(count):
+        take(w, 2, None)
+        give(w, 2, 0, 4)
+        give(w, 2, None, 1)
+        take(w, 4, None)
+        give(w, 4, 1, 2)
+        give(w, 4, None, 1)
+    for w in range(count):
+        for half in (0, 1):
+            take(w, 6, half)
+            give(w, 6, half, 1)
+    for own in locals_:
+        own.wait()
+    order = [count - 1] + list(range(count - 1))
+    for w in order:
+        for held in (1, 3, 5):
+            take(w, held, None)
+        for half in (0, 1):
+            take(w, 7, half)
+        if w == count - 1:
+            rows = fulls[w].shape[0]
+            place = vec_all.at[pl.ds(pl.multiple_of(z_me * rows, 8), rows), :]
+            own = pltpu.make_async_copy(fulls[w], place, local_sems.at[count])
+            own.start()
+            for hop in range(1, tensor_size):
+                sent.append(
+                    send(
+                        fulls[w],
+                        place,
+                        z_send.at[hop - 1],
+                        z_recv.at[hop - 1],
+                        {"tensor": lax.rem(z_me + hop, tensor_size)},
+                    )
+                )
+    rows = fulls[count - 1].shape[0]
+    for hop in range(1, tensor_size):
+        other = lax.rem(z_me + tensor_size - hop, tensor_size)
+        place = vec_all.at[pl.ds(pl.multiple_of(other * rows, 8), rows), :]
+        pltpu.make_async_copy(place, place, z_recv.at[hop - 1]).wait()
+    own.wait()
+    for copy in sent:
+        copy.wait_send()
+
+
+def gather_all(shards, axes, tensor_size):
+    count = len(shards)
+    sizes = []
+    for shard, axis in zip(shards, axes):
+        rows, columns = shard.shape
+        shape = (rows * 8, columns) if axis == 0 else (rows, columns * 8)
+        sizes.append(jax.ShapeDtypeStruct(shape, shard.dtype))
+    vec = sizes[-1]
+    outs = sizes + [jax.ShapeDtypeStruct((vec.shape[0] * tensor_size, LANES), vec.dtype)]
+    vmem = pl.BlockSpec(memory_space=pltpu.VMEM)
+    results = pl.pallas_call(
+        functools.partial(gather_kernel, axes, tensor_size),
+        out_shape=outs,
+        in_specs=[vmem] * count,
+        out_specs=[pl.BlockSpec(memory_space=pl.ANY)] * (count - 1) + [vmem, vmem],
+        scratch_shapes=[
+            pltpu.SemaphoreType.DMA((count, 9)),
+            pltpu.SemaphoreType.DMA((count, 9)),
+            pltpu.SemaphoreType.DMA((count + 1,)),
+            pltpu.SemaphoreType.DMA((tensor_size - 1,)),
+            pltpu.SemaphoreType.DMA((tensor_size - 1,)),
+        ],
+        compiler_params=pltpu.CompilerParams(collective_id=0, has_side_effects=True),
+        cost_estimate=pl.CostEstimate(
+            flops=20_000_000_000, bytes_accessed=80_000_000, transcendentals=0
+        ),
+    )(*shards)
+    return list(results[: count - 1]) + [results[count]]
+
+
+def reduce_kernel(axes, tensor_size, with_vec, *refs):
+    count = len(axes)
+    terms, outs = list(refs[:count]), refs[count : 2 * count]
+    scratch = refs[2 * count :]
+    from_core, sums, from_x, from_y = (
+        scratch[n * count : (n + 1) * count] for n in range(4)
+    )
+    half_in = scratch[4 * count : 5 * count]
+    send_sems, recv_sems = scratch[5 * count : 5 * count + 2]
+    peer, z_me = enter(tensor_size if with_vec else 1)
+    sent = []
+
+    def give(w, source, target, slot, to):
+        sent.append(
+            send(source, target, send_sems.at[w, slot], recv_sems.at[w, slot], {"dp": peer[to]})
+        )
+
+    def take(w, target, slot):
+        pltpu.make_async_copy(target, target, recv_sems.at[w, slot]).wait()
+
+    def first(w):
+        for k in (3, 1, 2, 0):
+            give(w, part(terms[w], peer[1 ^ (2 * k)], axes[w]), from_core[w].at[k], k, 1)
+
+    if with_vec:
+        vec_in, vec_sum, z_send, z_recv = scratch[5 * count + 2 :]
+        rows = vec_sum.shape[0]
+        for hop in range(1, tensor_size):
+            other = lax.rem(z_me + hop, tensor_size)
+            sent.append(
+                send(
+                    terms[-1].at[pl.ds(pl.multiple_of(other * rows, 8), rows), :],
+                    vec_in.at[hop - 1],
+                    z_send.at[hop - 1],
+                    z_recv.at[hop - 1],
+                    {"tensor": other},
+                )
+            )
+    plain = count - 1 if with_vec else count
+    for w in range(plain):
+        first(w)
+    if with_vec:
+        total = terms[-1][pl.ds(pl.multiple_of(z_me * rows, 8), rows), :]
+        for hop in range(1, tensor_size):
+            pltpu.make_async_copy(
+                vec_in.at[hop - 1], vec_in.at[hop - 1], z_recv.at[hop - 1]
+            ).wait()
+            total = total + vec_in[hop - 1]
+        vec_sum[...] = total
+        terms[-1] = vec_sum
+        first(count - 1)
+
+    def halves(w):
+        length = sums[w].shape[1] // 2
+        return length, pl.ds(0, length), pl.ds(length, length)
+
+    for w in range(count):
+        length, low, high = halves(w)
+        for k in (3, 1, 2, 0):
+            take(w, from_core[w].at[k], k)
+            mine = part(terms[w], peer[2 * k], axes[w])[...]
+            sums[w][k] = (
+                mine.astype(jnp.float32) + from_core[w][k].astype(jnp.float32)
+            ).astype(sums[w].dtype)
+            if k == 3:
+                give(w, sums[w].at[3, low], half_in[w].at[0], 4, 2)
+                give(w, sums[w].at[3, high], half_in[w].at[1], 5, 4)
+            if k == 1:
+                give(w, sums[w].at[1, low], from_x[w].at[low], 6, 2)
+            if k == 2:
+                give(w, sums[w].at[2, high], from_y[w].at[high], 7, 4)
+    for w in range(count):
+        length, low, high = halves(w)
+        take(w, half_in[w].at[0], 4)
+        sums[w][2, low] = (
+            sums[w][2, low].astype(jnp.float32) + half_in[w][0].astype(jnp.float32)
+        ).astype(sums[w].dtype)
+        give(w, sums[w].at[2, low], from_y[w].at[low], 8, 4)
+        take(w, half_in[w].at[1], 5)
+        sums[w][1, high] = (
+            sums[w][1, high].astype(jnp.float32) + half_in[w][1].astype(jnp.float32)
+        ).astype(sums[w].dtype)
+        give(w, sums[w].at[1, high], from_x[w].at[high], 9, 2)
+    for w in range(count):
+        length, low, high = halves(w)
+        take(w, from_x[w].at[low], 6)
+        take(w, from_y[w].at[high], 7)
+        take(w, from_y[w].at[low], 8)
+        take(w, from_x[w].at[high], 9)
+        outs[w][...] = (
+            sums[w][0].astype(jnp.float32)
+            + from_x[w][...].astype(jnp.float32)
+            + from_y[w][...].astype(jnp.float32)
+        )
+    for copy in sent:
+        copy.wait_send()
+
+
+def reduce_all(terms, axes, tensor_size, with_vec, collective_id):
+    count = len(terms)
+    blocks = []
+    for n, (term, axis) in enumerate(zip(terms, axes)):
+        rows, columns = term.shape
+        if with_vec and n == count - 1:
+            rows = rows // tensor_size
+        blocks.append((rows // 8, columns) if axis == 0 else (rows, columns // 8))
+    kinds = [term.dtype for term in terms]
+    pairs = list(zip(blocks, kinds))
+    scratch = (
+        [pltpu.VMEM((4,) + block, kind) for block, kind in pairs]
+        + [pltpu.VMEM((4,) + block, kind) for block, kind in pairs]
+        + [pltpu.VMEM(block, kind) for block, kind in pairs]
+        + [pltpu.VMEM(block, kind) for block, kind in pairs]
+        + [pltpu.VMEM((2, block[0] // 2, block[1]), kind) for block, kind in pairs]
+        + [pltpu.SemaphoreType.DMA((count, 10)), pltpu.SemaphoreType.DMA((count, 10))]
+    )
+    if with_vec:
+        rows = terms[-1].shape[0] // tensor_size
+        scratch += [
+            pltpu.VMEM((tensor_size - 1, rows, LANES), jnp.float32),
+            pltpu.VMEM((rows, LANES), jnp.float32),
+            pltpu.SemaphoreType.DMA((tensor_size - 1,)),
+            pltpu.SemaphoreType.DMA((tensor_size - 1,)),
+        ]
+    vmem = pl.BlockSpec(memory_space=pltpu.VMEM)
+    return pl.pallas_call(
+        functools.partial(reduce_kernel, axes, tensor_size, with_vec),
+        out_shape=[jax.ShapeDtypeStruct(block, jnp.float32) for block in blocks],
+        in_specs=[vmem] * count,
+        out_specs=[vmem] * count,
+        scratch_shapes=scratch,
+        compiler_params=pltpu.CompilerParams(
+            collective_id=collective_id, has_side_effects=True
+        ),
+        cost_estimate=pl.CostEstimate(
+            flops=15_000_000_000, bytes_accessed=60_000_000, transcendentals=0
+        ),
+    )(*terms)
 
 
 def gather_weights(w_qkv, w_out, w_up, w_down):
@@ -162,7 +481,7 @@
     heads_here = head_cols // HEAD_DIM
     hidden_here = w_up.shape[1]
     tokens_full = gather_rows(tokens)
-    qkv_weight, out_weight, up_weight, down_weight = gather_weights(w_qkv, w_out, w_up, w_down)
+    use_kernels = lax.axis_size("dp") == 8 and members > 1
     pieces = (
         first_norm_gain_param,
         first_norm_bias,
@@ -174,7 +493,23 @@
         down_bias,
     )
     widths = [piece.shape[0] for piece in pieces]
-    packed = lax.all_gather(jnp.concatenate(pieces), ("dp", "tensor"), axis=0)
+    packed = jnp.concatenate(pieces)
+    length = packed.shape[0]
+    if use_kernels:
+        vec = jnp.zeros((VEC_ROWS * LANES,), jnp.float32).at[:length].set(packed)
+        qkv_weight, out_weight, up_weight, down_weight, everyone = gather_all(
+            (w_qkv, w_out, w_up, w_down, vec.reshape(VEC_ROWS, LANES)), (0, 1, 0, 1, 0), members
+        )
+        packed = (
+            everyone.reshape(members, 8, VEC_ROWS * LANES)[:, :, :length]
+            .transpose(1, 0, 2)
+            .reshape(8 * members, length)
+        )
+    else:
+        qkv_weight, out_weight, up_weight, down_weight = gather_weights(
+            w_qkv, w_out, w_up, w_down
+        )
+        packed = lax.all_gather(packed, ("dp", "tensor"), axis=0)
     ends = [sum(widths[: n + 1]) for n in range(len(widths))]
     (
         first_norm_gain,
@@ -223,6 +558,7 @@
     )
     mixed, logsum = per_slot(attend_slot, shaped)
     mixed_rows = mixed.reshape(group_rows, head_cols)
+    mixed_rows, grad_out_full = lax.optimization_barrier((mixed_rows, grad_out_full))
     attn_local = scatter_rows(jnp.dot(mixed_rows, out_weight, preferred_element_type=jnp.float32))
     residual_stream = layer_inputs + attn_local + out_shift
     second_normed_rows, second_standardized, second_inverse_deviation = apply_layer_norm(
@@ -231,18 +567,31 @@
     normed_two_full = gather_rows(second_normed_rows.astype(jnp.bfloat16))
     hidden = jnp.dot(normed_two_full, up_weight, preferred_element_type=jnp.float32) + up_local
     activated = gelu_value(hidden).astype(jnp.bfloat16)
-    mlp_local = scatter_rows(jnp.dot(activated, down_weight, preferred_element_type=jnp.float32))
-    output = (row_valid * (residual_stream + mlp_local + down_shift)).astype(jnp.bfloat16)
     down_term = left_product(activated, grad_out_full)
     hidden_gradient = right_product(grad_out_full, down_weight) * gelu_slope(hidden)
     grad_hidden_b = hidden_gradient.astype(jnp.bfloat16)
     up_term = left_product(normed_two_full, grad_hidden_b)
-    up_projection_gradient, down_projection_gradient = reduce_grads(up_term, down_term)
+    if use_kernels:
+        up_projection_gradient, down_projection_gradient = reduce_all(
+            (up_term.astype(jnp.bfloat16), down_term.astype(jnp.bfloat16)),
+            (0, 1),
+            members,
+            False,
+            1,
+        )
+    else:
+        up_projection_gradient, down_projection_gradient = reduce_grads(up_term, down_term)
     second_normed_gradient = scatter_rows(right_product(grad_hidden_b, up_weight))
     residual_gradient = output_gradient + layer_norm_backward(
         second_normed_gradient, second_standardized, second_inverse_deviation, second_norm_gain
     )
     grad_resid_full = gather_rows(residual_gradient.astype(jnp.bfloat16))
+    mlp_terms = jnp.dot(activated, down_weight, preferred_element_type=jnp.float32)
+    mlp_terms, grad_resid_full, up_projection_gradient = lax.optimization_barrier(
+        (mlp_terms.astype(jnp.bfloat16), grad_resid_full, up_projection_gradient)
+    )
+    mlp_local = scatter_rows(mlp_terms)
+    output = (row_valid * (residual_stream + mlp_local + down_shift)).astype(jnp.bfloat16)
     out_term = left_product(mixed_rows, grad_resid_full)
     grad_mixed = right_product(grad_resid_full, out_weight).astype(jnp.bfloat16)
     back_items = shaped + (
@@ -260,7 +609,6 @@
         .astype(jnp.bfloat16)
     )
     qkv_term = left_product(normed_full, grad_projected)
-    query_key_value_gradient, output_projection_gradient = reduce_grads(qkv_term, out_term)
     first_normed_terms = right_product(grad_projected, qkv_weight)
     first_normed_gradient = scatter_rows(first_normed_terms)
     layer_input_gradient = residual_gradient + layer_norm_backward(
@@ -272,7 +620,7 @@
             jnp.sum(grad_values, axis=0).reshape(head_cols),
         ]
     )
-    qv_term = lax.dynamic_update_slice_in_dim(
+    qv_bias_term = lax.dynamic_update_slice_in_dim(
         jnp.zeros((2 * D,), jnp.float32), qv_piece, member * 2 * head_cols, 0
     )
     up_bias_term = lax.dynamic_update_slice_in_dim(
@@ -281,7 +629,7 @@
     vector_terms = (
         jnp.sum(first_normed_terms * standardized_full, axis=0),
         jnp.sum(first_normed_terms, axis=0),
-        qv_term,
+        qv_bias_term,
         jnp.sum(residual_gradient, axis=0),
         jnp.sum(second_normed_gradient * second_standardized, axis=0),
         jnp.sum(second_normed_gradient, axis=0),
@@ -291,9 +639,26 @@
     packed_terms = jnp.concatenate(
         [term.reshape(-1, width) for term, width in zip(vector_terms, widths)], axis=1
     )
-    packed_grad = lax.psum_scatter(
-        packed_terms, ("dp", "tensor"), scatter_dimension=0, tiled=False
-    )
+    if use_kernels:
+        spread = jnp.pad(packed_terms, ((0, 0), (0, VEC_ROWS * LANES - length)))
+        spread = spread.reshape(8, members, VEC_ROWS, LANES).transpose(1, 0, 2, 3)
+        query_key_value_gradient, output_projection_gradient, packed_grad = reduce_all(
+            (
+                qkv_term.astype(jnp.bfloat16),
+                out_term.astype(jnp.bfloat16),
+                spread.reshape(members * 8 * VEC_ROWS, LANES),
+            ),
+            (0, 1, 0),
+            members,
+            True,
+            2,
+        )
+        packed_grad = packed_grad.reshape(-1)[:length]
+    else:
+        query_key_value_gradient, output_projection_gradient = reduce_grads(qkv_term, out_term)
+        packed_grad = lax.psum_scatter(
+            packed_terms, ("dp", "tensor"), scatter_dimension=0, tiled=False
+        )
     (
         gain_one_grad,
         shift_one_grad,

time: 584 us -> 322 us (0.55)
  waiting for transfers between devices: 340 us -> 127 us
  blocking collectives: 122 us -> 0 us
  Pallas kernels: 0 us -> 92.6 us
  matrix products: 59.9 us -> 47.3 us
    pallas_call x0 -> x3, Pallas kernels: none -> 92.6 us  [the longest x2 51.2 us: reduce_all(): pl.pallas_call(functools.partial(reduce_kernel, axes, tensor_size, with_v...]
    all_gather x2 -> x0, blocking collectives: 82.3 us -> none  [the longest x1 71.2 us: per_device(): packed = lax.all_gather(jnp.concatenate(pieces), ('dp', 'tensor'), axis=0)]
    reduce_scatter x2 -> x0, waiting for transfers between devices: 75.6 us -> none  [reduce_grads(): lax.psum_scatter(row_split.astype(jnp.bfloat16), 'dp', scatter_dimension=...]
    all_gather x3 -> x0, waiting for transfers between devices: 49 us -> none  [the longest x1 29.1 us: gather_weights(): lax.all_gather(w_down, 'dp', axis=1, tiled=True)]
    all_gather x4, waiting for transfers between devices: 79.6 us -> 39.8 us  [gather_rows(): return lax.all_gather(values, 'tensor', axis=0, tiled=True)]
    unnamed x1 -> x0, blocking collectives: 39.7 us -> none
    reduce_scatter x4, waiting for transfers between devices: 117 us -> 86.4 us  [scatter_rows(): lax.psum_scatter(values.astype(jnp.bfloat16), 'tensor', scatter_dimension...]
    unnamed x17 -> x8, waiting for transfers between devices: 18.4 us -> 0.8 us
  transfers between devices with their start and end apart: 15 -> 8, of which waited for: 12 -> 5; matrix products, arithmetic and copies ran while one was open for 13% -> 13% of each run, Pallas kernels for 0% -> 29%
where the time goes in v2:
time: 322 us
  waiting for transfers between devices  127 us (39%)
  Pallas kernels  92.6 us (29%)
  matrix products  47.3 us (15%)
  other arithmetic  24.1 us (7%)
  local copies, waits for them, and re-layouts  15.4 us (5%)
  between operations  14.6 us (5%)
    reduce_scatter x4, waiting for transfers between devices, scatter_rows(): lax.psum_scatter(values.astype(jnp.bfloat16), 'tensor', scatter_dimension...  86.4 us
    pallas_call x2, Pallas kernels, reduce_all(): pl.pallas_call(functools.partial(reduce_kernel, axes, tensor_size, with_v...  51.2 us
    pallas_call x1, Pallas kernels, gather_all(): pl.pallas_call(functools.partial(gather_kernel, axes, tensor_size), out_s...  41.5 us
    all_gather x4, waiting for transfers between devices, gather_rows(): return lax.all_gather(values, 'tensor', axis=0, tiled=True)  39.8 us
    dot_general x4, matrix products, left_product(): lax.dot_general(first, second, (((0,), (0,)), ((), ())), preferred_elemen...  14.2 us
    dot_general x4, matrix products, right_product(): lax.dot_general(first, second, (((1,), (1,)), ((), ())), preferred_elemen...  10.1 us
    unnamed x53, local copies, waits for them, and re-layouts  7.58 us
  transfers between devices with their start and end apart: 8, of which 5 were waited for; matrix products, arithmetic and copies ran while one was open for 13% of the time, Pallas kernels for 29%

profile of v2, /device:TPU:0, one launch (start us, length us, event | category | flops | bytes accessed | tf_op | source)
XLA Modules:
  0.0 321.7 jit_solution(11961945910902189267)
XLA Ops:
  9.9 1.9 multiply_convert_fusion.3
  14.0 41.5 %shard_map.254 = (bf16[1024,768]{1,0:T(8,128)(2,1)}, bf16[256,1024]{1,0:T(8,128)(2,1)}, bf16[1024,1024]{1,0:T(8,128)(2,1)}, bf16[1024,1024]{1,0:T(8,128)(2,1)}, f32[128,128]{1,0:T(8,128)}, /*index=5*/f32[512,128]{1,0:T(8,128)}) custom-call(bf16[128,768]{1,0:T(8,128)(2,1)} %refs_0_.1, bf16[256,128]{1,0:T(8,128)(2,1)} %refs_1_.1, bf16[128,1024]{1,0:T(8,128)(2,1)} %refs_2_.1, ...), custom_call_target="tpu_custom_call" | custom-call | flops 20000000000 | bytes 80000000 | tf_op jit(solution)/shard_map/pallas_call | solution.py:233
  57.3 1.7 convert_reduce_fusion
  59.0 1.8 fusion.9
  60.8 1.6 fusion.55
  62.5 1.7 fusion.1
  64.2 1.5 exponential_reduce_fusion
  66.9 1.5 fusion
  68.5 1.4 convolution_convert_fusion.9
  69.9 8.7 %all-gather.7.cloned.1.call-done = bf16[640,1024]{1,0:T(8,128)(2,1)} async-done(((bf16[160,1024]{1,0:T(8,128)(2,1)}), bf16[640,1024]{1,0:T(8,128)(2,1)}) %all-gather.7.cloned.1.call-update) | async-done | bytes 1310736 | tf_op jit(solution)/shard_map/all_gather | solution.py:69
  78.6 2.8 convolution_convert_fusion.3
  81.7 30.4 %reduce-scatter.5.cloned.1.call-done = bf16[160,1024]{1,0:T(8,128)(2,1)} async-done(((bf16[640,1024]{1,0:T(8,128)(2,1)}), bf16[160,1024]{1,0:T(8,128)(2,1)}) %reduce-scatter.5.cloned.1.call-update) | async-done | bytes 327696 | tf_op jit(solution)/shard_map/reduce_scatter | solution.py:73
  114.6 2.0 add_convert_fusion
  117.0 31.1 %all-gather.9.cloned.1.call-done = bf16[640,1024]{1,0:T(8,128)(2,1)} async-done(((bf16[160,1024]{1,0:T(8,128)(2,1)}), bf16[640,1024]{1,0:T(8,128)(2,1)}) %all-gather.9.cloned.1.call-update) | async-done | bytes 1310736 | tf_op jit(solution)/shard_map/all_gather | solution.py:69
  148.0 5.0 %multiply_convert_fusion.1 = (bf16[640,1024]{1,0:T(8,128)(2,1)}, f32[640,1024]{1,0:T(8,128)S(1)}) fusion(f32[1024]{0:T(1024)S(1)} %dynamic_slice.7, bf16[640,1024]{1,0:T(8,128)(2,1)} %all-gather.9.cloned.1.call-done, bf16[1024,1024]{1,0:T(8,128)(2,1)} %get-tuple-element.45), kind=kOutput, calls=%fused_computation.21 | convolution fusion | flops 1346109440 | bytes 7344128 | tf_op jit(solution)/shard_map/dot_general | solution.py:568
  153.0 2.6 fusion.65
  156.7 2.7 convolution_convert_fusion.4
  159.5 4.9 %convolution_convert_fusion.refs_1_ = bf16[1024,1024]{1,0:T(8,128)(2,1)} fusion(bf16[640,1024]{1,0:T(8,128)(2,1)} %get-tuple-element.92, bf16[640,1024]{1,0:T(8,128)(2,1)} %all-gather.7.cloned.1.call-done), kind=kOutput, calls=%fused_computation.23 | convolution fusion | flops 1343225856 | bytes 4718592 | tf_op jit(solution)/shard_map/dot_general | solution.py:57
  164.4 25.6 %reduce-scatter.7.cloned.1.call-done = bf16[160,1024]{1,0:T(8,128)(2,1)} async-done(((bf16[640,1024]{1,0:T(8,128)(2,1)}), bf16[160,1024]{1,0:T(8,128)(2,1)}) %reduce-scatter.7.cloned.1.call-update) | async-done | bytes 327696 | tf_op jit(solution)/shard_map/reduce_scatter | solution.py:73
  190.1 1.7 fusion.32
  191.8 1.9 fusion.58
  195.6 5.0 %convolution_convert_fusion.1.refs_0_ = bf16[1024,1024]{1,0:T(8,128)(2,1)} fusion(bf16[640,1024]{1,0:T(8,128)(2,1)} %all-gather.9.cloned.1.call-done, bf16[640,1024]{1,0:T(8,128)(2,1)} %copy-done.22), kind=kOutput, calls=%fused_computation.24 | convolution fusion | flops 1343225856 | bytes 4718592 | tf_op jit(solution)/shard_map/dot_general | solution.py:57
  200.6 2.6 convolution_convert_fusion.5
  203.2 24.6 %shard_map.255 = (f32[128,1024]{1,0:T(8,128)}, f32[1024,128]{1,0:T(8,128)}) custom-call(bf16[1024,1024]{1,0:T(8,128)(2,1)} %convolution_convert_fusion.1.refs_0_, bf16[1024,1024]{1,0:T(8,128)(2,1)} %convolution_convert_fusion.refs_1_), custom_call_target="tpu_custom_call" | custom-call | flops 15000000512 | bytes 60000000 | tf_op jit(solution)/shard_map/pallas_call | solution.py:378
  227.9 2.2 multiply_reduce_fusion
  231.6 4.8 %multiply_convert_fusion = bf16[4,640,640]{1,2,0:T(8,128)(2,1)S(1)} fusion(f32[4,640,640]{1,2,0:T(8,128)} %copy-done, f32[4,640]{1,0:T(4,128)S(1)} %bitcast.109, f32[4,640]{1,0:T(4,128)S(1)} %log_add_fusion, pred[640]{0:T(1024)(128)(4,1)S(1)} %fusion.51, bf16[640,4,64]{0,2,1:T(8,128)(2,1)S(1)} %bitcast.105, f32[640,3,4,64]{0,3,2,1:T(8,128)S(1)} %bitcast.96, ...), kind=kOutput, calls=%fused_computation | convolution fusion | flops 221511680 | bytes 10836992 | tf_op jit(solution)/shard_map/qhd,khd->hqk/dot_general | solution.py:441
  239.4 2.6 fusion.57
  244.4 2.9 convolution_convert_fusion.2.refs_0_
  247.3 1.4 convolution_convert_fusion.6.refs_1_
  248.6 26.5 %shard_map.256 = (f32[128,768]{1,0:T(8,128)}, f32[256,128]{1,0:T(8,128)}, f32[16,128]{1,0:T(8,128)}) custom-call(bf16[1024,768]{1,0:T(8,128)(2,1)} %convolution_convert_fusion.2.refs_0_, bf16[256,1024]{1,0:T(8,128)(2,1)} %convolution_convert_fusion.6.refs_1_, f32[512,128]{1,0:T(8,128)} %bitcast.106), custom_call_target="tpu_custom_call" | custom-call | flops 15000000512 | bytes 60000000 | tf_op jit(solution)/shard_map/pallas_call | solution.py:378
  279.0 30.4 %reduce-scatter.9.cloned.1.call-done = bf16[160,1024]{1,0:T(8,128)(2,1)} async-done(((bf16[640,1024]{1,0:T(8,128)(2,1)}), bf16[160,1024]{1,0:T(8,128)(2,1)}) %reduce-scatter.9.cloned.1.call-update) | async-done | bytes 327696 | tf_op jit(solution)/shard_map/reduce_scatter | solution.py:73
  309.5 2.4 fusion.25
  (133 shorter events, 27.7 us)
Async XLA Ops:
  7.2 50.1 %all-gather.5.cloned.1.call-start = ((), (), s32[]{:S(2)}) async-start(), calls=%async_computation.4 | async-start | bytes 1638400 | tf_op jit(solution)/shard_map/all_gather | solution.py:69
  7.9 70.7 %all-gather.7.cloned.1.call-start = ((), (), s32[]{:S(2)}) async-start(), calls=%async_computation.5 | async-start | bytes 1638400 | tf_op jit(solution)/shard_map/all_gather | solution.py:69
  11.9 100.2 %reduce-scatter.5.cloned.1.call-start = ((), (), s32[]{:S(2)}) async-start(), calls=%async_computation.6 | async-start | bytes 1638400 | tf_op jit(solution)/shard_map/reduce_scatter | solution.py:73
  55.5 5.3 %copy-start.16 = (bf16[1024,768]{1,0:T(8,128)(2,1)S(1)}, bf16[1024,768]{1,0:T(8,128)(2,1)}, u32[]{:S(2)}) copy-start(bf16[1024,768]{1,0:T(8,128)(2,1)} %get-tuple-element.42) | copy-start | bytes 4718596
  57.3 3.5 %copy-start.7 = (bf16[640,1024]{1,0:T(8,128)(2,1)S(1)}, bf16[640,1024]{1,0:T(8,128)(2,1)}, u32[]{:S(2)}) copy-start(bf16[640,1024]{1,0:T(8,128)(2,1)} %all-gather.5.cloned.1.call-done) | copy-start | bytes 3932164
  62.5 6.0 %copy-start.5 = (f32[640,768]{0,1:T(8,128)}, f32[640,768]{0,1:T(8,128)S(1)}, u32[]{:S(2)}) copy-start(f32[640,768]{0,1:T(8,128)S(1)} %fusion.55) | copy-start | bytes 5898244
  64.2 2.7 copy-start
  81.4 66.6 %all-gather.9.cloned.1.call-start = ((), (), s32[]{:S(2)}) async-start(), calls=%async_computation.7 | async-start | bytes 1638400 | tf_op jit(solution)/shard_map/all_gather | solution.py:69
  116.7 73.4 %reduce-scatter.7.cloned.1.call-start = ((), (), s32[]{:S(2)}) async-start(), calls=%async_computation.8 | async-start | bytes 1638400 | tf_op jit(solution)/shard_map/reduce_scatter | solution.py:73
  148.0 5.0 %copy-start.15 = (bf16[640,1024]{1,0:T(8,128)(2,1)S(1)}, bf16[640,1024]{1,0:T(8,128)(2,1)}, u32[]{:S(2)}) copy-start(bf16[640,1024]{1,0:T(8,128)(2,1)} %all-gather.7.cloned.1.call-done) | copy-start | bytes 3932164
  148.0 5.0 %copy-start.19 = (bf16[1024,1024]{1,0:T(8,128)(2,1)S(1)}, bf16[1024,1024]{1,0:T(8,128)(2,1)}, u32[]{:S(2)}) copy-start(bf16[1024,1024]{1,0:T(8,128)(2,1)} %get-tuple-element.46) | copy-start | bytes 6291460
  153.0 3.7 %copy-start.18 = (bf16[1024,1024]{1,0:T(8,128)(2,1)S(1)}, bf16[1024,1024]{1,0:T(8,128)(2,1)}, u32[]{:S(2)}) copy-start(bf16[1024,1024]{1,0:T(8,128)(2,1)} %get-tuple-element.45) | copy-start | bytes 6291460
  155.6 1.1 copy-start.22
  159.4 68.4 %all-gather.11.cloned.1.call-start = ((), (), s32[]{:S(2)}) async-start(), calls=%async_computation.9 | async-start | bytes 1638400 | tf_op jit(solution)/shard_map/all_gather | solution.py:69
  193.7 0.8 copy-start.3
  195.3 82.4 %reduce-scatter.11.cloned.1.call-start = ((), (), s32[]{:S(2)}) async-start(), calls=%async_computation.11 | async-start | bytes 1638400 | tf_op jit(solution)/shard_map/reduce_scatter | solution.py:73
  195.6 5.0 %copy-start.20 = (bf16[1024,1024]{1,0:T(8,128)(2,1)S(1)}, bf16[1024,1024]{1,0:T(8,128)(2,1)}, u32[]{:S(2)}) copy-start(bf16[1024,1024]{1,0:T(8,128)(2,1)} %get-tuple-element.46) | copy-start | bytes 6291460
  195.6 5.0 %copy-start.21 = (bf16[640,1024]{1,0:T(8,128)(2,1)S(1)}, bf16[640,1024]{1,0:T(8,128)(2,1)}, u32[]{:S(2)}) copy-start(bf16[640,1024]{1,0:T(8,128)(2,1)} %get-tuple-element.92) | copy-start | bytes 3932164
  230.1 1.5 copy-start.6
  237.6 1.3 copy-start.8
  237.6 1.8 copy-start.17
  242.0 67.4 %reduce-scatter.9.cloned.1.call-start = ((), (), s32[]{:S(2)}) async-start(), calls=%async_computation.10 | async-start | bytes 1638400 | tf_op jit(solution)/shard_map/reduce_scatter | solution.py:73
  244.3 2.9 copy-start.9
  244.4 2.9 copy-start.10
  248.6 29.1 %copy-start.1 = (bf16[160,1024]{1,0:T(8,128)(2,1)S(1)}, bf16[160,1024]{1,0:T(8,128)(2,1)}, u32[]{:S(2)}) copy-start(bf16[160,1024]{1,0:T(8,128)(2,1)} %param.17) | copy-start | bytes 983044
  248.6 60.8 %copy-start.2 = (bf16[160,1024]{1,0:T(8,128)(2,1)S(1)}, bf16[160,1024]{1,0:T(8,128)(2,1)}, u32[]{:S(2)}) copy-start(bf16[160,1024]{1,0:T(8,128)(2,1)} %reduce-scatter.5.cloned.1.call-done) | copy-start | bytes 983044
  248.6 60.8 %copy-start.4 = (f32[160,1024]{1,0:T(8,128)S(1)}, f32[160,1024]{1,0:T(8,128)}, u32[]{:S(2)}) copy-start(f32[160,1024]{1,0:T(8,128)} %copy-done.3) | copy-start | bytes 1966084
  275.2 36.6 %copy-start.13 = (f32[128,768]{1,0:T(8,128)S(1)}, f32[128,768]{1,0:T(8,128)}, u32[]{:S(2)}) copy-start(f32[128,768]{1,0:T(8,128)} %get-tuple-element.121) | copy-start | bytes 1179652
  275.2 37.4 %copy-start.14 = (f32[256,128]{1,0:T(8,128)S(1)}, f32[256,128]{1,0:T(8,128)}, u32[]{:S(2)}) copy-start(f32[256,128]{1,0:T(8,128)} %get-tuple-element.123) | copy-start | bytes 393220
  275.2 38.0 %copy-start.12 = (f32[128,1024]{1,0:T(8,128)S(1)}, f32[128,1024]{1,0:T(8,128)}, u32[]{:S(2)}) copy-start(f32[128,1024]{1,0:T(8,128)} %get-tuple-element.127) | copy-start | bytes 1572868
  279.0 35.1 %copy-start.11 = (f32[1024,128]{1,0:T(8,128)S(1)}, f32[1024,128]{1,0:T(8,128)}, u32[]{:S(2)}) copy-start(f32[1024,128]{1,0:T(8,128)} %get-tuple-element.129) | copy-start | bytes 1572868
Sparse Core Ops, SparseCore 0:
  9.6 35.2 all-gather.4
  47.0 31.6 all-gather.6
  81.6 30.4 reduce-scatter.4
  116.8 31.1 all-gather.8
  159.6 30.4 reduce-scatter.6
  195.4 31.1 all-gather.10
  242.2 34.3 reduce-scatter.10
  278.9 30.5 reduce-scatter.8
